TPU v7x, 256 devices: a whole 4x4x8 slice. The times are simulated.
256 devices in a mesh: seq: 32 (over y, z), head: 8 (over x, core).
Axes of the slice: x: 4, y: 4, z: 8, core: 2. Of those that a mesh axis runs over, the one named last changes fastest.
Arguments:
- block_input: bfloat16 [4096, 3072], P('seq'), may hold values from -12 to 12
- grad_output: bfloat16 [4096, 3072], P('seq'), may hold values from -6 to 6
- weights: bfloat16 [3072, 4, 3072], P('seq', None, 'head'), may hold values from -0.109375 to 0.109375
- clip_ids: int32 [32], replicated, may hold values from 0 to 2, never falling along the last dimension, each value on 1 to 16 neighbouring positions
Outputs:
- grad_input: bfloat16 [4096, 3072], P('seq', 'head')
- grad_weights: bfloat16 [3072, 4, 3072], P('seq', None, 'head')
Inputs may be any that keep to these rules, and one draw needn't show every extreme that they name: `clip_ids`: clip numbers never fall from one frame to the next; every clip number of 0 to 2 is used, each clip spans 1 to 16 frames and one spans exactly 16.
All inputs are finite; a program needn't handle non-finite values.
Results may differ from a plain program's by a relative error of at most 0.018.
Values may be sent and summed in bfloat16 or wider, within the bound.
No kernel may reach another device: no remote copies, remote signals or barrier semaphores. Data moves between devices by JAX's collectives and lax.ppermute only.
A program may use at most 128 MiB of HBM per device.

v0:
```python
import jax
import jax.numpy as jnp
from jax import lax
from jax.sharding import Mesh
from jax.sharding import PartitionSpec as P

HD = 128
WIN = 1
P_SIZE = 128
SEQ = ("seq_0", "seq_1")
big_negative = -1e30


def padded(cells, sides, width):
    for axis, dim in sides:
        count = lax.axis_size(axis)
        ends = count - 1
        head = lax.slice_in_dim(cells, 0, width, axis=dim)
        tail = lax.slice_in_dim(cells, cells.shape[dim] - width, cells.shape[dim], axis=dim)
        cells = jnp.concatenate(
            [
                lax.ppermute(tail, axis, [(i, (i + 1) % count) for i in range(ends)]),
                cells,
                lax.ppermute(head, axis, [((i + 1) % count, i) for i in range(ends)]),
            ],
            axis=dim,
        )
    return cells


def split_up(x, dim, count):
    before, after = (x.shape[:dim], x.shape[dim + 1 :])
    return jnp.moveaxis(x.reshape(*before, count, -1, *after), dim, 0)


def piece_ends(length, count):
    unit = 8 if length >= 8 * count else 1
    return [length // unit * k // count * unit for k in range(1, count)]


def own_block(pieces, axes, sequence):
    inside = pieces.shape[1:]
    pieces = pieces.reshape(*(lax.axis_size(a) for a in axes), *inside)
    pieces = jnp.moveaxis(pieces, sequence, range(len(axes))).reshape(-1, *inside)
    for k in sequence:
        pieces = lax.psum_scatter(pieces, axes[k], scatter_dimension=0, tiled=True)
    return pieces[0]


def spread_scatter(x, axes, dim):
    pieces = split_up(x, dim, lax.axis_size(axes))
    widest = max(range(1, max(2, pieces.ndim - 1)), key=lambda d: pieces.shape[d])
    count, outs = (len(axes), [])
    for first, section in enumerate(
        jnp.split(pieces, piece_ends(pieces.shape[widest], count), axis=widest)
    ):
        if section.size:
            sequence = [(first + k) % count for k in range(count)]
            outs.append(own_block(section, axes, sequence))
    return jnp.concatenate(outs, axis=widest - 1)


def sent_and_summed(x, axis, dim):
    pieces = split_up(x, dim, lax.axis_size(axis))
    arrived = lax.all_to_all(pieces, axis, split_axis=0, concat_axis=0, tiled=True)
    return arrived.astype(jnp.float32).sum(axis=0)


def attend(query_rows, key_ext, value_ext, grad_rows, clip_ext):
    frame_count = clip_ext.shape[0] - 2 * WIN
    window_len = 2 * WIN + 1
    head_count = query_rows.shape[1] // HD
    score_scale = HD ** (-0.5)
    query_frames = query_rows.reshape(frame_count, P_SIZE, head_count, HD)
    key_frames = key_ext.reshape(frame_count + 2 * WIN, P_SIZE, head_count, HD)
    value_frames = value_ext.reshape(frame_count + 2 * WIN, P_SIZE, head_count, HD)
    grad_frames = grad_rows.reshape(frame_count, P_SIZE, head_count, HD)
    key_window = jnp.stack(
        [key_frames[offset : offset + frame_count] for offset in range(window_len)], axis=1
    )
    value_window = jnp.stack(
        [value_frames[offset : offset + frame_count] for offset in range(window_len)], axis=1
    )
    clip_window = jnp.stack(
        [clip_ext[offset : offset + frame_count] for offset in range(window_len)], axis=1
    )
    allowed = clip_window == clip_ext[WIN : WIN + frame_count][:, None]
    allowed = allowed[:, None, None, :, None]
    scores = (
        jnp.einsum(
            "fihc,fojhc->fhioj", query_frames, key_window, preferred_element_type=jnp.float32
        )
        * score_scale
    )
    masked = jnp.where(allowed, scores, big_negative)
    top_score = jnp.max(masked, axis=(3, 4), keepdims=True)
    expo_terms = jnp.where(allowed, jnp.exp(masked - top_score), 0.0)
    attn_prob = expo_terms / jnp.sum(expo_terms, axis=(3, 4), keepdims=True)
    prob_low = attn_prob.astype(jnp.bfloat16)
    attn_out = jnp.einsum(
        "fhioj,fojhc->fihc", prob_low, value_window, preferred_element_type=jnp.float32
    )
    delta_row = jnp.sum(grad_frames.astype(jnp.float32) * attn_out, axis=3)
    delta_row = jnp.transpose(delta_row, (0, 2, 1))[:, :, :, None, None]
    grad_prob = jnp.einsum(
        "fihc,fojhc->fhioj", grad_frames, value_window, preferred_element_type=jnp.float32
    )
    grad_score = (attn_prob * (grad_prob - delta_row)).astype(jnp.bfloat16)
    grad_query = (
        jnp.einsum("fhioj,fojhc->fihc", grad_score, key_window, preferred_element_type=jnp.float32)
        * score_scale
    )
    grad_key_window = (
        jnp.einsum(
            "fhioj,fihc->fojhc", grad_score, query_frames, preferred_element_type=jnp.float32
        )
        * score_scale
    )
    grad_value_window = jnp.einsum(
        "fhioj,fihc->fojhc", prob_low, grad_frames, preferred_element_type=jnp.float32
    )
    grad_key = jnp.zeros((frame_count + 2 * WIN, P_SIZE, head_count, HD), jnp.float32)
    grad_value = jnp.zeros((frame_count + 2 * WIN, P_SIZE, head_count, HD), jnp.float32)
    for offset in range(window_len):
        grad_key = grad_key.at[offset : offset + frame_count].add(grad_key_window[:, offset])
        grad_value = grad_value.at[offset : offset + frame_count].add(grad_value_window[:, offset])
    column_count = head_count * HD
    return (
        grad_query.reshape(frame_count * P_SIZE, column_count),
        grad_key.reshape((frame_count + 2 * WIN) * P_SIZE, column_count),
        grad_value.reshape((frame_count + 2 * WIN) * P_SIZE, column_count),
        attn_out.astype(jnp.bfloat16).reshape(frame_count * P_SIZE, column_count),
    )


def on_device(block_input, grad_output, weights, clip_ids):
    row_count = block_input.shape[0]
    feature_count = block_input.shape[1]
    slab_rows = weights.shape[0]
    column_count = weights.shape[2]
    frame_count = row_count // P_SIZE
    rim_rows = WIN * P_SIZE
    seq_index = lax.axis_index(SEQ)
    full_weights = lax.all_gather(weights, SEQ, axis=0, tiled=True)
    projected = jnp.dot(
        block_input,
        full_weights[:, :3].reshape(feature_count, 3 * column_count),
        preferred_element_type=jnp.float32,
    )
    grad_attn = jnp.dot(grad_output, full_weights[:, 3], preferred_element_type=jnp.float32)
    projected = projected.astype(jnp.bfloat16)
    grad_attn = grad_attn.astype(jnp.bfloat16)
    query_rows = projected[:, :column_count]
    key_value = jnp.stack(
        [projected[:, column_count : 2 * column_count], projected[:, 2 * column_count :]]
    )
    extended = padded(key_value, ((SEQ, 1),), rim_rows)
    clip_rim = jnp.full((WIN,), -1, jnp.int32)
    clip_padded = jnp.concatenate([clip_rim, clip_ids, clip_rim])
    clip_ext = lax.dynamic_slice_in_dim(
        clip_padded, seq_index * frame_count, frame_count + 2 * WIN, 0
    )
    grad_query, grad_key, grad_value, attn_low = attend(
        query_rows, extended[0], extended[1], grad_attn, clip_ext
    )
    grad_pair = jnp.stack([grad_key, grad_value])
    lower_rim = grad_pair[:, :rim_rows]
    upper_rim = grad_pair[:, rim_rows + row_count :]
    inner_rows = grad_pair[:, rim_rows : rim_rows + row_count]
    both_rims = jnp.concatenate([lower_rim, upper_rim], axis=1)
    beside_all = padded(both_rims, ((SEQ, 1),), rim_rows)
    from_below = beside_all[:, :rim_rows]
    from_above = beside_all[:, 3 * rim_rows :]
    inner_rows = inner_rows.at[:, :rim_rows].add(from_below)
    inner_rows = inner_rows.at[:, row_count - rim_rows :].add(from_above)
    grad_qkv = jnp.concatenate([grad_query, inner_rows[0], inner_rows[1]], axis=1).astype(
        jnp.bfloat16
    )
    grad_weights = (
        spread_scatter(
            jnp.concatenate(
                [
                    lax.dot_general(
                        block_input,
                        grad_qkv,
                        (((0,), (0,)), ((), ())),
                        preferred_element_type=jnp.float32,
                    ).reshape(slab_rows * lax.axis_size(SEQ), 3, column_count),
                    lax.dot_general(
                        grad_output,
                        attn_low,
                        (((0,), (0,)), ((), ())),
                        preferred_element_type=jnp.float32,
                    )[:, None, :],
                ],
                axis=1,
            ).astype(jnp.bfloat16),
            SEQ,
            0,
        )
        .astype(jnp.float32)
        .astype(jnp.bfloat16)
    )
    partial_input = lax.dot_general(
        grad_qkv,
        full_weights[:, :3].reshape(feature_count, 3 * column_count),
        (((1,), (1,)), ((), ())),
        preferred_element_type=jnp.float32,
    )
    grad_input = sent_and_summed(partial_input.astype(jnp.bfloat16), "head", 1).astype(jnp.bfloat16)
    return (grad_input, grad_weights)


def solution(mesh):
    torus = Mesh(mesh.devices.reshape(4, 8, mesh.shape["head"]), ("seq_0", "seq_1", "head"))
    return jax.shard_map(
        on_device,
        mesh=torus,
        in_specs=(P(SEQ, None), P(SEQ, None), P(SEQ, None, "head"), P()),
        out_specs=(P(SEQ, "head"), P(SEQ, None, "head")),
        check_vma=False,
    )
```

profile of v0, /device:TPU:2, one launch (start us, length us, event | category | flops | bytes accessed | tf_op | source)
XLA Modules:
  0.0 428.7 jit_solution(6999756514082008056)
XLA Ops:
  7.2 0.7 all-gather.2.cloned.1.call-update
  8.0 0.7 pad_add_fusion
  8.8 0.6 slice.299
  9.4 0.7 broadcast_compare_fusion
  10.1 106.7 %all-gather.2.cloned.1.call-done = bf16[3072,4,384]{2,1,0:T(4,128)(2,1)} async-done(((bf16[96,4,384]{2,1,0:T(4,128)(2,1)}), bf16[3072,4,384]{2,1,0:T(4,128)(2,1)}) %all-gather.2.cloned.1.call-update) | async-done | bytes 9437200 | tf_op jit(solution)/shard_map/all_gather | solution.py:144
  116.7 14.5 %copy.165 = bf16[3072,3,384]{0,2,1:T(8,128)(2,1)} copy(bf16[3072,3,384]{2,1,0:T(4,128)(2,1)} %bitcast.151) | data formatting | bytes 14155776
  131.2 5.3 %convolution_convert_fusion.3 = bf16[128,1152]{1,0:T(8,128)(2,1)S(1)} fusion(bf16[128,3072]{1,0:T(8,128)(2,1)S(1)} %copy-done, bf16[3072,1152]{0,1:T(8,128)(2,1)} %bitcast.149), kind=kOutput, calls=%fused_computation.8 | convolution fusion | flops 906117120 | bytes 8159232 | tf_op jit(solution)/shard_map/dot_general | solution.py:145
  136.7 1.4 collective-permute-start.1
  138.1 6.8 %slice.323 = bf16[3072,1,384]{2,1,0:T(2,128)(2,1)S(1)} slice(bf16[3072,4,384]{2,1,0:T(4,128)(2,1)} %all-gather.2.cloned.1.call-done), slice={[0:3072], [3:4], [0:384]} | slice | bytes 4718592 | tf_op jit(solution)/shard_map/slice | solution.py:150
  144.9 0.6 fusion.9
  145.5 0.1 copy.119
  145.6 0.1 copy.127
  145.7 4.6 %collective-permute-start = (bf16[2,128,384]{2,1,0:T(8,128)(2,1)S(1)}, bf16[2,128,384]{2,1,0:T(8,128)(2,1)S(1)}, u32[]{:S(2)}, u32[]{:S(2)}) collective-permute-start(bf16[2,128,384]{2,1,0:T(8,128)(2,1)S(1)} %pad_maximum_fusion.4), channel_id=1, source_target_pairs={{0,8},{8,16},{16,24},{24,32},{32,40},{40,48},{48,56},{56,64},{64,7... | collective-permute-start | bytes 589832 | tf_op jit(solution)/shard_map/ppermute | solution.py:22
  150.3 0.1 copy.111
  150.4 0.1 copy.114
  150.6 0.1 copy.116
  150.7 0.1 copy.121
  150.8 0.1 copy.124
  151.0 0.1 copy.112
  151.1 0.1 copy.115
  151.3 0.1 copy.122
  151.4 0.1 copy.125
  151.5 1.9 collective-permute-done
  153.5 0.1 copy.110
  153.6 0.1 copy.113
  153.7 0.1 copy.120
  153.9 0.1 copy.123
  154.0 0.2 fusion.35
  154.3 0.1 fusion.10
  154.4 0.2 fusion.12
  154.6 0.4 convolution_bitcast_fusion
  155.0 1.0 fusion.32
  156.1 0.3 fusion.6
  156.4 0.2 fusion.5
  156.8 0.3 copy-done.7
  157.2 0.3 copy.141
  157.5 0.3 stack_reshape.7
  158.0 0.4 copy.137
  158.4 0.3 stack_reshape.6
  158.8 1.0 copy-done.2
  159.8 1.0 fusion.30
  160.8 5.1 %collective-permute-start.2 = (f32[2,128,384]{2,1,0:T(8,128)}, f32[2,128,384]{2,1,0:T(8,128)}, u32[]{:S(2)}, u32[]{:S(2)}) collective-permute-start(f32[2,128,384]{2,1,0:T(8,128)} %get-tuple-element.122), channel_id=1, source_target_pairs={{0,8},{8,16},{16,24},{24,32},{32,40},{40,48},{48,56},{56,64},{64,7... | collective-permute-start | bytes 1179656 | tf_op jit(solution)/shard_map/ppermute | solution.py:22
  165.9 1.5 collective-permute-start.3
  167.4 1.4 fusion.8
  168.8 0.1 copy.142
  168.9 2.0 fusion.2
  170.9 2.4 copy.144
  173.3 4.9 %copy.145 = bf16[32,96,1,384]{1,0,3,2:T(8,128)(2,1)} copy(bf16[32,96,1,384]{3,1,0,2:T(8,128)(2,1)} %bitcast.153) | data formatting | bytes 4718592 | tf_op jit(solution)/shard_map/concatenate | solution.py:181
  178.3 1.3 fusion.14
  179.6 4.9 %fusion.1 = bf16[3072,1152]{0,1:T(8,128)(2,1)} fusion(bf16[128,3072]{1,0:T(8,128)(2,1)S(1)} %copy-done, bf16[128,384]{1,0:T(8,128)(2,1)S(1)} %get-tuple-element.132, bf16[128,384]{1,0:T(8,128)(2,1)S(1)} %get-tuple-element.131, bf16[128,384]{1,0:T(8,128)(2,1)S(1)} %copy.142), kind=kOutput, calls=%fused_computation.4 | convolution fusion | flops 910393344 | bytes 8159232 | tf_op jit(solution)/shard_map/dot_general | solution.py:183
  184.5 15.7 %concatenate.45 = bf16[32,96,3,384]{1,0,3,2:T(8,128)(2,1)} reshape(bf16[3072,1152]{0,1:T(8,128)(2,1)} %fusion.1) | data formatting | bytes 14155776 | tf_op jit(solution)/shard_map/concatenate | solution.py:181
  200.2 20.5 %slice_maximum_fusion = (bf16[32,48,4,384]{1,0,3,2:T(8,128)(2,1)}, bf16[8,4,48,4,384]{2,0,1,4,3:T(8,128)(2,1)}) fusion(bf16[32,96,1,384]{1,0,3,2:T(8,128)(2,1)} %copy.145, bf16[32,96,3,384]{1,0,3,2:T(8,128)(2,1)} %concatenate.45), kind=kLoop, calls=%fused_computation.2 | loop fusion | flops 18874368 | bytes 18874368 | tf_op jit(solution)/shard_map/concatenate | solution.py:181
  220.7 14.1 %copy.147 = bf16[8,4,48,4,384]{4,2,3,1,0:T(8,128)(2,1)} copy(bf16[8,4,48,4,384]{2,0,1,4,3:T(8,128)(2,1)} %get-tuple-element.121) | data formatting | bytes 9437184 | tf_op jit(solution)/shard_map/transpose | solution.py:44
  234.8 14.1 %copy.146 = bf16[32,48,4,384]{3,1,2,0:T(8,128)(2,1)} copy(bf16[32,48,4,384]{1,0,3,2:T(8,128)(2,1)} %get-tuple-element.120) | data formatting | bytes 9437184 | tf_op jit(solution)/shard_map/split | solution.py:55
  248.9 48.2 %reduce-scatter.9.cloned.1.call-done = bf16[4,48,4,384]{3,1,2,0:T(8,128)(2,1)} async-done(((bf16[32,48,4,384]{3,1,2,0:T(8,128)(2,1)}), bf16[4,48,4,384]{3,1,2,0:T(8,128)(2,1)}) %reduce-scatter.9.cloned.1.call-update) | async-done | bytes 589840 | tf_op jit(solution)/shard_map/reduce_scatter | solution.py:46
  297.2 54.8 %reduce-scatter.5.cloned.1.call-done = bf16[8,48,4,384]{3,1,2,0:T(8,128)(2,1)} async-done(((bf16[32,48,4,384]{3,1,2,0:T(8,128)(2,1)}), bf16[8,48,4,384]{3,1,2,0:T(8,128)(2,1)}) %reduce-scatter.5.cloned.1.call-update) | async-done | bytes 1179664 | tf_op jit(solution)/shard_map/reduce_scatter | solution.py:46
  352.1 4.3 convolution_convert_fusion.2
  356.4 0.1 copy.177
  356.5 16.3 %all_to_all.5 = bf16[8,128,384]{2,1,0:T(8,128)(2,1)S(1)} all-to-all(bf16[8,128,384]{2,1,0:T(8,128)(2,1)S(1)} %bitcast.159), channel_id=1, replica_groups=mesh['seq_0'=4,'seq_1'=8,'head'=8] {'head'}, dimensions={0} | all-to-all | bytes 1572864 | tf_op jit(solution)/shard_map/all_to_all | solution.py:65
  372.8 0.8 reduce_sum.35
  373.6 5.1 %reduce-scatter.11.cloned.1.call-done = bf16[1,48,4,384]{3,1,2,0:T(8,128)(2,1)} async-done(((bf16[4,48,4,384]{3,1,2,0:T(8,128)(2,1)}), bf16[1,48,4,384]{3,1,2,0:T(8,128)(2,1)}) %reduce-scatter.11.cloned.1.call-update) | async-done | bytes 147472 | tf_op jit(solution)/shard_map/reduce_scatter | solution.py:46
  378.6 41.6 %reduce-scatter.7.cloned.1.call-done = bf16[1,48,4,384]{3,1,2,0:T(8,128)(2,1)} async-done(((bf16[8,48,4,384]{3,1,2,0:T(8,128)(2,1)}), bf16[1,48,4,384]{3,1,2,0:T(8,128)(2,1)}) %reduce-scatter.7.cloned.1.call-update) | async-done | bytes 147472 | tf_op jit(solution)/shard_map/reduce_scatter | solution.py:46
  420.3 1.0 pad_maximum_fusion.3
  421.3 0.9 copy.148
  (43 shorter events, 0.9 us)
Async XLA Ops:
  7.2 124.1 %copy-start = (bf16[128,3072]{1,0:T(8,128)(2,1)S(1)}, bf16[128,3072]{1,0:T(8,128)(2,1)}, u32[]{:S(2)}) copy-start(bf16[128,3072]{1,0:T(8,128)(2,1)} %param.24) | copy-start | bytes 2359300
  7.2 109.6 %all-gather.2.cloned.1.call-start = ((), (), s32[]{:S(2)}) async-start(), calls=%async_computation.5 | async-start | bytes 9732096 | tf_op jit(solution)/shard_map/all_gather | solution.py:144
  7.9 289.2 %reduce-scatter.9.cloned.1.call-start = ((), (), s32[]{:S(2)}) async-start(), calls=%async_computation.8 | async-start | bytes 5308416 | tf_op jit(solution)/shard_map/reduce_scatter | solution.py:46
  136.6 8.3 %copy-start.3 = (bf16[128,3072]{1,0:T(8,128)(2,1)S(1)}, bf16[128,3072]{1,0:T(8,128)(2,1)}, u32[]{:S(2)}) copy-start(bf16[128,3072]{1,0:T(8,128)(2,1)} %param.25) | copy-start | bytes 2359300
  136.7 14.3 %collective-permute-start.1 = (bf16[2,128,384]{2,1,0:T(8,128)(2,1)S(1)}, bf16[2,128,384]{2,1,0:T(8,128)(2,1)S(1)}, u32[]{:S(2)}, u32[]{:S(2)}) collective-permute-start(bf16[2,128,384]{2,1,0:T(8,128)(2,1)S(1)} %pad_maximum_fusion.4), channel_id=1, source_target_pairs={{8,0},{16,8},{24,16},{32,24},{40,32},{48,40},{56,48},{64,56},{72,6... | collective-permute-start | bytes 589832 | tf_op jit(solution)/shard_map/ppermute | solution.py:24
  145.7 7.7 %collective-permute-start = (bf16[2,128,384]{2,1,0:T(8,128)(2,1)S(1)}, bf16[2,128,384]{2,1,0:T(8,128)(2,1)S(1)}, u32[]{:S(2)}, u32[]{:S(2)}) collective-permute-start(bf16[2,128,384]{2,1,0:T(8,128)(2,1)S(1)} %pad_maximum_fusion.4), channel_id=1, source_target_pairs={{0,8},{8,16},{16,24},{24,32},{32,40},{40,48},{48,56},{56,64},{64,7... | collective-permute-start | bytes 589832 | tf_op jit(solution)/shard_map/ppermute | solution.py:22
  150.6 5.8 %copy-start.4 = (bf16[1,1,128,3,128]{4,2,1,3,0:T(8,128)(2,1)}, bf16[1,1,128,3,128]{4,2,1,3,0:T(8,128)(2,1)S(1)}, u32[]{:S(2)}) copy-start(bf16[1,1,128,3,128]{4,2,1,3,0:T(8,128)(2,1)S(1)} %copy.114) | copy-start | bytes 294916
  151.3 5.2 %copy-start.5 = (bf16[1,1,128,3,128]{4,2,1,3,0:T(8,128)(2,1)}, bf16[1,1,128,3,128]{4,2,1,3,0:T(8,128)(2,1)S(1)}, u32[]{:S(2)}) copy-start(bf16[1,1,128,3,128]{4,2,1,3,0:T(8,128)(2,1)S(1)} %copy.115) | copy-start | bytes 294916
  153.7 2.7 copy-start.6
  156.4 0.7 copy-start.7
  158.8 1.0 copy-start.2
  160.8 17.5 %collective-permute-start.2 = (f32[2,128,384]{2,1,0:T(8,128)}, f32[2,128,384]{2,1,0:T(8,128)}, u32[]{:S(2)}, u32[]{:S(2)}) collective-permute-start(f32[2,128,384]{2,1,0:T(8,128)} %get-tuple-element.122), channel_id=1, source_target_pairs={{0,8},{8,16},{16,24},{24,32},{32,40},{40,48},{48,56},{56,64},{64,7... | collective-permute-start | bytes 1179656 | tf_op jit(solution)/shard_map/ppermute | solution.py:22
  165.9 12.4 %collective-permute-start.3 = (f32[2,128,384]{2,1,0:T(8,128)}, f32[2,128,384]{2,1,0:T(8,128)}, u32[]{:S(2)}, u32[]{:S(2)}) collective-permute-start(f32[2,128,384]{2,1,0:T(8,128)} %get-tuple-element.123), channel_id=1, source_target_pairs={{8,0},{16,8},{24,16},{32,24},{40,32},{48,40},{56,48},{64,56},{72,6... | collective-permute-start | bytes 1179656 | tf_op jit(solution)/shard_map/ppermute | solution.py:24
  234.7 117.3 %reduce-scatter.5.cloned.1.call-start = ((), (), s32[]{:S(2)}) async-start(), calls=%async_computation.6 | async-start | bytes 5898240 | tf_op jit(solution)/shard_map/reduce_scatter | solution.py:46
  248.9 129.7 %reduce-scatter.11.cloned.1.call-start = ((), (), s32[]{:S(2)}) async-start(), calls=%async_computation.9 | async-start | bytes 737280 | tf_op jit(solution)/shard_map/reduce_scatter | solution.py:46
  297.2 123.1 %reduce-scatter.7.cloned.1.call-start = ((), (), s32[]{:S(2)}) async-start(), calls=%async_computation.7 | async-start | bytes 1327104 | tf_op jit(solution)/shard_map/reduce_scatter | solution.py:46
  352.1 70.0 %copy-start.1 = (bf16[128,3072]{1,0:T(8,128)(2,1)S(1)}, bf16[128,3072]{1,0:T(8,128)(2,1)}, u32[]{:S(2)}) copy-start(bf16[128,3072]{1,0:T(8,128)(2,1)} %param.24) | copy-start | bytes 2359300
Sparse Core Ops, SparseCore 0:
  10.6 106.1 all-gather.1
  234.9 62.2 reduce-scatter.8
  299.7 52.3 reduce-scatter.4
  354.5 24.1 reduce-scatter.10
  381.0 39.1 reduce-scatter.6
where the time goes:
time: 431 us; the launch traced here: 429 us
  waiting for transfers between devices  259 us (60%)
  local copies, waits for them, and re-layouts  80.1 us (19%)
  other arithmetic  25.5 us (6%)
  matrix products  20.7 us (5%)
  blocking collectives  16.3 us (4%)
  between operations  14.2 us (3%)
  starting transfers between devices  12.8 us (3%)
    reduce_scatter x4, waiting for transfers between devices, own_block(): pieces = lax.psum_scatter(pieces, axes[k], scatter_dimension=0, tiled=True)  150 us
    all_gather x1, waiting for transfers between devices, on_device(): full_weights = lax.all_gather(weights, SEQ, axis=0, tiled=True)  107 us
    concatenate x2, local copies, waits for them, and re-layouts, on_device(): jnp.concatenate([lax.dot_general(block_input, grad_qkv, (((0,), (0,)), ((...  20.6 us
    concatenate x1, other arithmetic, on_device(): jnp.concatenate([lax.dot_general(block_input, grad_qkv, (((0,), (0,)), ((...  20.5 us
    unnamed x19, local copies, waits for them, and re-layouts  16.8 us
    all_to_all x1, blocking collectives, sent_and_summed(): lax.all_to_all(pieces, axis, split_axis=0, concat_axis=0, tiled=True)  16.3 us
    split x1, local copies, waits for them, and re-layouts, spread_scatter(): jnp.split(pieces, piece_ends(pieces.shape[widest], count), axis=widest)  14.1 us
    transpose x1, local copies, waits for them, and re-layouts, own_block(): jnp.moveaxis(pieces, sequence, range(len(axes))).reshape(-1, *inside)  14.1 us
  transfers between devices with their start and end apart: 9, of which 6 were waited for; matrix products, arithmetic and copies ran while one was open for 10% of the time, Pallas kernels for 0%

commit v1 on v0

--- a/solution.py
+++ b/solution.py
@@ -141,7 +141,9 @@
     frame_count = row_count // P_SIZE
     rim_rows = WIN * P_SIZE
     seq_index = lax.axis_index(SEQ)
-    full_weights = lax.all_gather(weights, SEQ, axis=0, tiled=True)
+    full_weights = jnp.concatenate(
+        lax.all_to_all(jnp.stack([weights] * lax.axis_size(SEQ)), SEQ, 0, 0), axis=0
+    )
     projected = jnp.dot(
         block_input,
         full_weights[:, :3].reshape(feature_count, 3 * column_count),

time: 431 us -> 569 us (1.32)
  waiting for transfers between devices: 259 us -> 373 us
  starting transfers between devices: 12.8 us -> 26.4 us
  local copies, waits for them, and re-layouts: 80.1 us -> 90.3 us
    all_to_all x0 -> x1, waiting for transfers between devices: none -> 212 us  [on_device(): lax.all_to_all(jnp.stack([weights] * lax.axis_size(SEQ)), SEQ, 0, 0)]
    all_gather x1 -> x0, waiting for transfers between devices: 107 us -> none  [on_device(): full_weights = lax.all_gather(weights, SEQ, axis=0, tiled=True)]
    unnamed x19 -> x21, local copies, waits for them, and re-layouts: 16.8 us -> 3.39 us
    all_to_all x0 -> x1, starting transfers between devices: none -> 11.7 us  [on_device(): lax.all_to_all(jnp.stack([weights] * lax.axis_size(SEQ)), SEQ, 0, 0)]
    slice x1 -> x2, local copies, waits for them, and re-layouts: 6.76 us -> 16.8 us  [on_device(): full_weights[:, :3].reshape(feature_count, 3 * column_count)]
    all_to_all x0 -> x1, local copies, waits for them, and re-layouts: none -> 8.52 us  [on_device(): lax.all_to_all(jnp.stack([weights] * lax.axis_size(SEQ)), SEQ, 0, 0)]
    reduce_scatter x4, waiting for transfers between devices: 150 us -> 158 us  [own_block(): pieces = lax.psum_scatter(pieces, axes[k], scatter_dimension=0, tiled=True)]
  transfers between devices with their start and end apart: 9 -> 9, of which waited for: 6 -> 7; matrix products, arithmetic and copies ran while one was open for 10% -> 6% of each run, Pallas kernels for 0% -> 0%
where the time goes in v1:
time: 569 us; the launch traced here: 568 us
  waiting for transfers between devices  373 us (66%)
  local copies, waits for them, and re-layouts  90.3 us (16%)
  starting transfers between devices  26.4 us (5%)
  other arithmetic  24.8 us (4%)
  matrix products  22.5 us (4%)
  blocking collectives  16.3 us (3%)
  between operations  14.2 us (2%)
    all_to_all x1, waiting for transfers between devices, on_device(): lax.all_to_all(jnp.stack([weights] * lax.axis_size(SEQ)), SEQ, 0, 0)  212 us
    reduce_scatter x4, waiting for transfers between devices, own_block(): pieces = lax.psum_scatter(pieces, axes[k], scatter_dimension=0, tiled=True)  158 us
    concatenate x2, local copies, waits for them, and re-layouts, on_device(): jnp.concatenate([lax.dot_general(block_input, grad_qkv, (((0,), (0,)), ((...  20.6 us
    concatenate x1, other arithmetic, on_device(): jnp.concatenate([lax.dot_general(block_input, grad_qkv, (((0,), (0,)), ((...  20.5 us
    slice x2, local copies, waits for them, and re-layouts, on_device(): full_weights[:, :3].reshape(feature_count, 3 * column_count)  16.8 us
    all_to_all x1, blocking collectives, sent_and_summed(): lax.all_to_all(pieces, axis, split_axis=0, concat_axis=0, tiled=True)  16.3 us
    split x1, local copies, waits for them, and re-layouts, spread_scatter(): jnp.split(pieces, piece_ends(pieces.shape[widest], count), axis=widest)  14.1 us
    transpose x1, local copies, waits for them, and re-layouts, own_block(): jnp.moveaxis(pieces, sequence, range(len(axes))).reshape(-1, *inside)  14.1 us
  transfers between devices with their start and end apart: 9, of which 7 were waited for; matrix products, arithmetic and copies ran while one was open for 6% of the time, Pallas kernels for 0%

profile of v1, /device:TPU:2, one launch (start us, length us, event | category | flops | bytes accessed | tf_op | source)
XLA Modules:
  0.0 567.5 jit_solution(6111918666446514028)
XLA Ops:
  7.2 1.1 copy.109
  8.3 5.1 stack.26
  13.3 11.7 %all-to-all-start = ((bf16[32,96,4,384]{3,1,2,0:T(8,128)(2,1)}), bf16[32,96,4,384]{3,1,2,0:T(8,128)(2,1)}, u32[]{:S(2)}, u32[]{:S(2)}) async-start(bf16[32,96,4,384]{3,1,2,0:T(8,128)(2,1)} %stack.26), calls=%async_computation | async-start | bytes 18874368 | tf_op jit(solution)/shard_map/all_to_all | solution.py:145
  25.3 0.6 slice.299
  25.9 0.7 broadcast_compare_fusion
  26.6 212.3 %all-to-all-done = bf16[32,96,4,384]{3,1,2,0:T(8,128)(2,1)} async-done(((bf16[32,96,4,384]{3,1,2,0:T(8,128)(2,1)}), bf16[32,96,4,384]{3,1,2,0:T(8,128)(2,1)}, u32[]{:S(2)}, u32[]{:S(2)}) %all-to-all-start) | async-done | bytes 9437216 | tf_op jit(solution)/shard_map/all_to_all | solution.py:145
  238.9 8.5 %copy.110 = bf16[32,96,4,384]{3,1,0,2:T(8,128)(2,1)} copy(bf16[32,96,4,384]{3,1,2,0:T(8,128)(2,1)} %all-to-all-done) | data formatting | bytes 18874368 | tf_op jit(solution)/shard_map/all_to_all | solution.py:145
  247.4 6.5 %slice.317 = bf16[3072,3,384]{2,0,1:T(8,128)(2,1)} slice(bf16[3072,4,384]{2,0,1:T(8,128)(2,1)} %bitcast.151), slice={[0:3072], [0:3], [0:384]} | slice | bytes 14155776 | tf_op jit(solution)/shard_map/slice | solution.py:149
  254.0 10.3 %copy.111 = bf16[3072,3,384]{0,2,1:T(8,128)(2,1)} copy(bf16[3072,3,384]{2,0,1:T(8,128)(2,1)} %slice.317) | data formatting | bytes 14155776 | tf_op jit(solution)/shard_map/slice | solution.py:149
  264.3 5.4 convolution_convert_fusion.3
  269.8 1.3 collective-permute-start.1
  271.1 2.3 fusion.9
  273.4 0.1 copy.120
  273.6 6.7 %collective-permute-start = (bf16[2,128,384]{2,1,0:T(8,128)(2,1)S(1)}, bf16[2,128,384]{2,1,0:T(8,128)(2,1)S(1)}, u32[]{:S(2)}, u32[]{:S(2)}) collective-permute-start(bf16[2,128,384]{2,1,0:T(8,128)(2,1)S(1)} %pad_maximum_fusion.4), channel_id=1, source_target_pairs={{0,8},{8,16},{16,24},{24,32},{32,40},{40,48},{48,56},{56,64},{64,7... | collective-permute-start | bytes 589832 | tf_op jit(solution)/shard_map/ppermute | solution.py:22
  280.3 0.1 copy.113
  280.4 0.1 copy.116
  280.6 0.1 copy.118
  280.7 0.1 copy.122
  280.8 0.1 copy.125
  281.0 0.1 copy.114
  281.1 0.1 copy.117
  281.3 0.1 copy.123
  281.4 0.1 copy.126
  281.5 2.2 collective-permute-done
  283.7 0.1 copy.112
  283.9 0.1 copy.115
  284.1 0.1 copy.124
  284.3 0.2 fusion.35
  284.5 0.1 fusion.10
  284.7 0.2 fusion.12
  284.9 0.4 convolution_bitcast_fusion
  285.3 1.0 fusion.32
  286.3 0.3 fusion.6
  286.7 0.2 fusion.5
  287.1 0.3 copy-done.7
  287.5 0.3 copy.142
  287.8 0.3 stack_reshape.7
  288.2 0.4 copy.138
  288.7 0.3 stack_reshape.6
  289.1 1.0 copy-done.2
  290.1 1.0 fusion.30
  291.1 5.1 collective-permute-start.2
  296.2 1.5 collective-permute-start.3
  297.6 1.4 fusion.8
  299.1 0.1 copy.143
  299.2 2.0 fusion.2
  301.2 2.4 copy.145
  303.6 4.9 copy.146
  308.5 0.4 collective-permute-done.3
  308.9 1.3 fusion.14
  310.3 4.9 fusion.1
  315.2 15.7 %concatenate.45 = bf16[32,96,3,384]{1,0,3,2:T(8,128)(2,1)} reshape(bf16[3072,1152]{0,1:T(8,128)(2,1)} %fusion.1) | data formatting | bytes 14155776 | tf_op jit(solution)/shard_map/concatenate | solution.py:183
  330.9 20.5 %slice_maximum_fusion = (bf16[32,48,4,384]{1,0,3,2:T(8,128)(2,1)}, bf16[8,4,48,4,384]{2,0,1,4,3:T(8,128)(2,1)}) fusion(bf16[32,96,1,384]{1,0,3,2:T(8,128)(2,1)} %copy.146, bf16[32,96,3,384]{1,0,3,2:T(8,128)(2,1)} %concatenate.45), kind=kLoop, calls=%fused_computation.2 | loop fusion | flops 18874368 | bytes 18874368 | tf_op jit(solution)/shard_map/concatenate | solution.py:183
  351.3 14.1 %copy.148 = bf16[8,4,48,4,384]{4,2,3,1,0:T(8,128)(2,1)} copy(bf16[8,4,48,4,384]{2,0,1,4,3:T(8,128)(2,1)} %get-tuple-element.121) | data formatting | bytes 9437184 | tf_op jit(solution)/shard_map/transpose | solution.py:44
  365.5 14.1 %copy.147 = bf16[32,48,4,384]{3,1,2,0:T(8,128)(2,1)} copy(bf16[32,48,4,384]{1,0,3,2:T(8,128)(2,1)} %get-tuple-element.120) | data formatting | bytes 9437184 | tf_op jit(solution)/shard_map/split | solution.py:55
  379.6 56.3 %reduce-scatter.9.cloned.1.call-done = bf16[4,48,4,384]{3,1,2,0:T(8,128)(2,1)} async-done(((bf16[32,48,4,384]{3,1,2,0:T(8,128)(2,1)}), bf16[4,48,4,384]{3,1,2,0:T(8,128)(2,1)}) %reduce-scatter.9.cloned.1.call-update) | async-done | bytes 589840 | tf_op jit(solution)/shard_map/reduce_scatter | solution.py:46
  436.0 54.8 %reduce-scatter.5.cloned.1.call-done = bf16[8,48,4,384]{3,1,2,0:T(8,128)(2,1)} async-done(((bf16[32,48,4,384]{3,1,2,0:T(8,128)(2,1)}), bf16[8,48,4,384]{3,1,2,0:T(8,128)(2,1)}) %reduce-scatter.5.cloned.1.call-update) | async-done | bytes 1179664 | tf_op jit(solution)/shard_map/reduce_scatter | solution.py:46
  490.8 4.3 convolution_convert_fusion.2
  495.2 16.3 %all_to_all.10 = bf16[8,128,384]{2,1,0:T(8,128)(2,1)S(1)} all-to-all(bf16[8,128,384]{2,1,0:T(8,128)(2,1)S(1)} %bitcast.160), channel_id=1, replica_groups=mesh['seq_0'=4,'seq_1'=8,'head'=8] {'head'}, dimensions={0} | all-to-all | bytes 1572864 | tf_op jit(solution)/shard_map/all_to_all | solution.py:65
  511.5 0.8 reduce_sum.35
  512.3 5.2 reduce-scatter.11.cloned.1.call-done
  517.5 41.6 %reduce-scatter.7.cloned.1.call-done = bf16[1,48,4,384]{3,1,2,0:T(8,128)(2,1)} async-done(((bf16[8,48,4,384]{3,1,2,0:T(8,128)(2,1)}), bf16[1,48,4,384]{3,1,2,0:T(8,128)(2,1)}) %reduce-scatter.7.cloned.1.call-update) | async-done | bytes 147472 | tf_op jit(solution)/shard_map/reduce_scatter | solution.py:46
  559.1 1.0 pad_maximum_fusion.3
  560.1 0.9 copy.149
  (47 shorter events, 1.2 us)
Async XLA Ops:
  7.2 257.1 %copy-start = (bf16[128,3072]{1,0:T(8,128)(2,1)S(1)}, bf16[128,3072]{1,0:T(8,128)(2,1)}, u32[]{:S(2)}) copy-start(bf16[128,3072]{1,0:T(8,128)(2,1)} %param.24) | copy-start | bytes 2359300
  13.3 11.8 %copy-start.8 = (s32[32]{0:T(128)S(1)}, s32[32]{0:T(128)}, u32[]{:S(2)}) copy-start(s32[32]{0:T(128)} %param.27) | copy-start | bytes 388
  13.3 225.6 %all-to-all-start = ((bf16[32,96,4,384]{3,1,2,0:T(8,128)(2,1)}), bf16[32,96,4,384]{3,1,2,0:T(8,128)(2,1)}, u32[]{:S(2)}, u32[]{:S(2)}) async-start(bf16[32,96,4,384]{3,1,2,0:T(8,128)(2,1)} %stack.26), calls=%async_computation | async-start | bytes 18874368 | tf_op jit(solution)/shard_map/all_to_all | solution.py:145
  25.1 410.8 %reduce-scatter.9.cloned.1.call-start = ((), (), s32[]{:S(2)}) async-start(), calls=%async_computation.8 | async-start | bytes 5308416 | tf_op jit(solution)/shard_map/reduce_scatter | solution.py:46
  264.3 6.8 %copy-start.3 = (bf16[128,3072]{1,0:T(8,128)(2,1)S(1)}, bf16[128,3072]{1,0:T(8,128)(2,1)}, u32[]{:S(2)}) copy-start(bf16[128,3072]{1,0:T(8,128)(2,1)} %param.25) | copy-start | bytes 2359300
  269.8 11.2 %collective-permute-start.1 = (bf16[2,128,384]{2,1,0:T(8,128)(2,1)S(1)}, bf16[2,128,384]{2,1,0:T(8,128)(2,1)S(1)}, u32[]{:S(2)}, u32[]{:S(2)}) collective-permute-start(bf16[2,128,384]{2,1,0:T(8,128)(2,1)S(1)} %pad_maximum_fusion.4), channel_id=1, source_target_pairs={{8,0},{16,8},{24,16},{32,24},{40,32},{48,40},{56,48},{64,56},{72,6... | collective-permute-start | bytes 589832 | tf_op jit(solution)/shard_map/ppermute | solution.py:24
  273.6 10.1 %collective-permute-start = (bf16[2,128,384]{2,1,0:T(8,128)(2,1)S(1)}, bf16[2,128,384]{2,1,0:T(8,128)(2,1)S(1)}, u32[]{:S(2)}, u32[]{:S(2)}) collective-permute-start(bf16[2,128,384]{2,1,0:T(8,128)(2,1)S(1)} %pad_maximum_fusion.4), channel_id=1, source_target_pairs={{0,8},{8,16},{16,24},{24,32},{32,40},{40,48},{48,56},{56,64},{64,7... | collective-permute-start | bytes 589832 | tf_op jit(solution)/shard_map/ppermute | solution.py:22
  280.6 6.1 %copy-start.4 = (bf16[1,1,128,3,128]{4,2,1,3,0:T(8,128)(2,1)}, bf16[1,1,128,3,128]{4,2,1,3,0:T(8,128)(2,1)S(1)}, u32[]{:S(2)}) copy-start(bf16[1,1,128,3,128]{4,2,1,3,0:T(8,128)(2,1)S(1)} %copy.116) | copy-start | bytes 294916
  281.3 5.4 copy-start.5
  284.0 2.7 copy-start.6
  286.7 0.7 copy-start.7
  289.1 1.0 copy-start.2
  291.1 17.5 %collective-permute-start.2 = (f32[2,128,384]{2,1,0:T(8,128)}, f32[2,128,384]{2,1,0:T(8,128)}, u32[]{:S(2)}, u32[]{:S(2)}) collective-permute-start(f32[2,128,384]{2,1,0:T(8,128)} %get-tuple-element.122), channel_id=1, source_target_pairs={{0,8},{8,16},{16,24},{24,32},{32,40},{40,48},{48,56},{56,64},{64,7... | collective-permute-start | bytes 1179656 | tf_op jit(solution)/shard_map/ppermute | solution.py:22
  296.2 12.8 %collective-permute-start.3 = (f32[2,128,384]{2,1,0:T(8,128)}, f32[2,128,384]{2,1,0:T(8,128)}, u32[]{:S(2)}, u32[]{:S(2)}) collective-permute-start(f32[2,128,384]{2,1,0:T(8,128)} %get-tuple-element.123), channel_id=1, source_target_pairs={{8,0},{16,8},{24,16},{32,24},{40,32},{48,40},{56,48},{64,56},{72,6... | collective-permute-start | bytes 1179656 | tf_op jit(solution)/shard_map/ppermute | solution.py:24
  365.4 125.4 %reduce-scatter.5.cloned.1.call-start = ((), (), s32[]{:S(2)}) async-start(), calls=%async_computation.6 | async-start | bytes 5898240 | tf_op jit(solution)/shard_map/reduce_scatter | solution.py:46
  379.6 138.0 %reduce-scatter.11.cloned.1.call-start = ((), (), s32[]{:S(2)}) async-start(), calls=%async_computation.9 | async-start | bytes 737280 | tf_op jit(solution)/shard_map/reduce_scatter | solution.py:46
  435.9 123.2 %reduce-scatter.7.cloned.1.call-start = ((), (), s32[]{:S(2)}) async-start(), calls=%async_computation.7 | async-start | bytes 1327104 | tf_op jit(solution)/shard_map/reduce_scatter | solution.py:46
  490.8 70.2 %copy-start.1 = (bf16[128,3072]{1,0:T(8,128)(2,1)S(1)}, bf16[128,3072]{1,0:T(8,128)(2,1)}, u32[]{:S(2)}) copy-start(bf16[128,3072]{1,0:T(8,128)(2,1)} %param.24) | copy-start | bytes 2359300
Sparse Core Ops, SparseCore 0:
  365.5 70.3 reduce-scatter.8
  438.4 52.3 reduce-scatter.4
  493.3 24.1 reduce-scatter.10
  519.9 39.1 reduce-scatter.6
